TPU v7x, 256 devices: a whole 4x4x8 slice. The times are simulated.
256 devices in a mesh: dp: 2 (over core), width: 4 (over x), vocab: 32 (over z, y).
Axes of the slice: x: 4, y: 4, z: 8, core: 2. Of those that a mesh axis runs over, the one named last changes fastest.
Arguments:
- hidden: bfloat16 [1024, 8192], P('dp', 'width'), may hold values from -68 to 68
- head: bfloat16 [8192, 2, 32064], P('width', 'dp', 'vocab'), may hold values from -0.25 to 0.25
- teacher: bfloat16 [1024, 2, 32064], P('dp', None, 'vocab'), may hold values from -180 to 180
Outputs:
- divergence: float32 [1024], P('dp')
- grad_head: bfloat16 [8192, 2, 32064], P('width', 'dp', 'vocab')
- grad_hidden: bfloat16 [1024, 8192], P('dp', 'width')
All inputs are finite; a program needn't handle non-finite values.
Results may differ from a plain program's by a relative error of at most 0.0052.
Values may be sent and summed in bfloat16 or wider, within the bound.
A program may use at most 128 MiB of HBM per device.

v0:
```python
import jax
import jax.numpy as jnp
from jax import lax
from jax.sharding import PartitionSpec as P

VOCAB = 64128


def body(hidden, head, teacher):
    tok_rows, width_cols = hidden.shape
    halves = teacher.shape[1]
    local_cols = teacher.shape[2]
    full_head = lax.all_gather(head, "dp", axis=1, tiled=True).reshape(
        width_cols, halves * local_cols
    )
    partial_value = jnp.dot(hidden, full_head, preferred_element_type=jnp.float32)
    student = lax.psum(partial_value, "width")
    target = teacher.reshape(tok_rows, halves * local_cols).astype(jnp.float32)
    student_peak = jnp.max(student, axis=1)
    target_peak = jnp.max(target, axis=1)
    student_peak, target_peak = lax.pmax((student_peak, target_peak), "vocab")
    target_exp = jnp.exp(target - target_peak[:, None])
    student_total, target_total, cross_total = lax.psum(
        (
            jnp.sum(jnp.exp(student - student_peak[:, None]), axis=1),
            jnp.sum(target_exp, axis=1),
            jnp.sum(target_exp * (target - student), axis=1),
        ),
        "vocab",
    )
    student_lse = student_peak + jnp.log(student_total)
    target_lse = target_peak + jnp.log(target_total)
    divergence = cross_total / target_total - target_lse + student_lse
    prob_student = jnp.exp(student - student_lse[:, None])
    prob_target = jnp.exp(target - target_lse[:, None])
    grad = (VOCAB * (prob_student - prob_target)).astype(jnp.bfloat16)
    grad_blocks = grad.reshape(tok_rows, halves, local_cols)
    blocks = width_cols * lax.axis_size("dp") // width_cols
    term = jnp.einsum("td,tkv->kdv", hidden, grad_blocks, preferred_element_type=jnp.float32)
    head_term = lax.psum_scatter(
        term.reshape(blocks * width_cols, local_cols), "dp", scatter_dimension=0, tiled=True
    )
    grad_head = head_term.astype(jnp.bfloat16).reshape(width_cols, 1, local_cols)
    hidden_term = lax.dot_general(
        grad, full_head, (((1,), (1,)), ((), ())), preferred_element_type=jnp.float32
    )
    grad_hidden = lax.psum(hidden_term, "vocab").astype(jnp.bfloat16)
    return (divergence, grad_head, grad_hidden)


def solution(mesh):
    return jax.shard_map(
        body,
        mesh=mesh,
        in_specs=(P("dp", "width"), P("width", "dp", "vocab"), P("dp", None, "vocab")),
        out_specs=(P("dp"), P("width", "dp", "vocab"), P("dp", "width")),
        check_vma=False,
    )
```

profile of v0, /device:TPU:2, one launch (start us, length us, event | category | flops | bytes accessed | tf_op | source)
XLA Modules:
  0.0 548.4 jit_solution(12567613389792812008)
XLA Ops:
  7.2 0.0 copy-start
  7.2 0.0 all-gather.2.cloned.1.call-start
  7.2 0.7 all-gather.2.cloned.1.call-update
  7.9 0.0 all-reduce.6.cloned.1.call-start
  8.0 29.8 %all-gather.2.cloned.1.call-done = bf16[2048,2,1002]{0,2,1:T(8,128)(2,1)} async-done(((bf16[2048,1,1002]{0,2,1:T(8,128)(2,1)}), bf16[2048,2,1002]{0,2,1:T(8,128)(2,1)}) %all-gather.2.cloned.1.call-update) | async-done | bytes 8208400 | tf_op jit(solution)/shard_map/all_gather | solution.py:13
  37.8 8.1 %reshape.29 = bf16[2048,2004]{0,1:T(8,128)(2,1)} reshape(bf16[2048,2,1002]{0,2,1:T(8,128)(2,1)} %all-gather.2.cloned.1.call-done) | data formatting | bytes 16416768 | tf_op jit(solution)/shard_map/reshape | solution.py:13
  45.9 0.0 copy-done
  45.9 8.8 %fusion.1 = f32[512,2004]{0,1:T(8,128)} fusion(bf16[512,2048]{1,0:T(8,128)(2,1)S(1)} %copy-done, bf16[2048,2004]{0,1:T(8,128)(2,1)} %reshape.29), kind=kOutput, calls=%fused_computation.10 | convolution fusion | flops 4202692608 | bytes 14409728 | tf_op jit(solution)/shard_map/dot_general | solution.py:16
  54.7 0.0 all-reduce.6.cloned.1.call-update
  54.7 0.0 reduce-scatter.2.cloned.1.call-start
  54.7 4.2 copy.13
  58.9 3.3 reduce_max.23
  62.2 4.5 reshape.33
  66.7 84.9 %all-reduce.6.cloned.1.call-done = f32[512,2004]{0,1:T(8,128)} async-done(((f32[512,2004]{0,1:T(8,128)}), f32[512,2004]{0,1:T(8,128)}) %all-reduce.6.cloned.1.call-update) | async-done | bytes 4104208 | tf_op jit(solution)/shard_map/psum | solution.py:17
  151.7 2.5 reduce_max.25
  154.2 75.3 %all-reduce.2 = (f32[512]{0:T(512)S(1)}, f32[512]{0:T(512)S(1)}) all-reduce(f32[512]{0:T(512)S(1)} %reduce_max.25, bf16[512]{0:T(512)(128)(2,1)S(1)} %reduce_max.23), channel_id=1, replica_groups=mesh['dp'=2,'width'=4,'vocab'=32] {'vocab'}, use_global_device_ids=true, to_apply=%region_8.0 | all-reduce | flops 1024 | bytes 7168 | tf_op jit(solution)/shard_map/pmax | solution.py:21
  229.4 4.9 exponential_reduce_fusion.1
  234.3 4.8 multiply_reduce_fusion
  239.1 69.6 %all-reduce.1 = (f32[512]{0:T(512)S(1)}, f32[512]{0:T(512)S(1)}) all-reduce(f32[512]{0:T(512)S(1)} %get-tuple-element.13, f32[512]{0:T(512)S(1)} %exponential_reduce_fusion.1), channel_id=1, replica_groups=mesh['dp'=2,'width'=4,'vocab'=32] {'vocab'}, use_global_device_ids=true, to_apply=%region_10.0 | all-reduce | flops 1024 | bytes 8192 | tf_op jit(solution)/shard_map/psum | solution.py:23
  308.7 5.9 %multiply_convert_fusion = bf16[512,2004]{0,1:T(8,128)(2,1)} fusion(f32[512,2004]{0,1:T(8,128)} %reshape.33, f32[512,2004]{0,1:T(8,128)} %all-reduce.6.cloned.1.call-done, f32[512]{0:T(512)S(1)} %get-tuple-element.21, f32[512]{0:T(512)S(1)} %get-tuple-element.20), kind=kLoop, calls=%fused_computation.2 | loop fusion | flops 5130240 | bytes 10264576 | tf_op jit(solution)/shard_map/convert_element_type | solution.py:36
  314.6 3.3 reshape.30
  317.9 9.5 %convolution_bitcast_fusion = f32[2,2048,1002]{1,2,0:T(8,128)} fusion(bf16[512,2,1002]{0,2,1:T(8,128)(2,1)} %reshape.30, bf16[512,2048]{1,0:T(8,128)(2,1)S(1)} %copy-done), kind=kOutput, calls=%fused_computation | convolution fusion | flops 4202692608 | bytes 20566016 | tf_op jit(solution)/shard_map/td,tkv->kdv/dot_general | solution.py:39
  327.4 17.9 %copy.14 = f32[2,2048,1002]{2,1,0:T(8,128)} copy(f32[2,2048,1002]{1,2,0:T(8,128)} %convolution_bitcast_fusion) | data formatting | bytes 32833536 | tf_op jit(solution)/shard_map/td,tkv->kdv/transpose | solution.py:39
  345.3 0.0 copy-start.2
  345.3 0.0 reduce-scatter.2.cloned.1.call-update
  345.4 1.6 copy-done.2
  346.9 9.5 %fusion.2 = f32[512,2048]{1,0:T(8,128)} fusion(bf16[512,2004]{0,1:T(8,128)(2,1)S(1)} %copy-done.2, bf16[2048,2004]{0,1:T(8,128)(2,1)} %reshape.29), kind=kOutput, calls=%fused_computation.11 | convolution fusion | flops 4202692608 | bytes 14454784 | tf_op jit(solution)/shard_map/dot_general | solution.py:44
  356.4 172.3 %all-reduce.7 = (f32[512]{0:T(512)S(1)}, bf16[512,2048]{1,0:T(8,128)(2,1)}) all-reduce(f32[512]{0:T(512)S(1)} %get-tuple-element.12, f32[512,2048]{1,0:T(8,128)} %fusion.2), channel_id=1, replica_groups=mesh['dp'=2,'width'=4,'vocab'=32] {'vocab'}, use_global_device_ids=true, to_apply=%region_4.0 | all-reduce | flops 1049088 | bytes 6295552 | tf_op jit(solution)/shard_map/psum | solution.py:23
  528.7 0.6 subtract_add_fusion
  529.3 0.0 reduce-scatter.2.cloned.1.call-done
  529.3 0.0 copy-start.1
  529.3 6.1 %convert_bitcast_fusion = bf16[2048,1,1002]{2,0,1:T(8,128)(2,1)} fusion(f32[2048,1002]{1,0:T(8,128)} %reduce-scatter.2.cloned.1.call-done), kind=kLoop, calls=%fused_computation.1 | loop fusion | flops 2052096 | bytes 12312576 | tf_op jit(solution)/shard_map/reshape | solution.py:43
  535.4 6.5 %copy.15 = bf16[2048,1,1002]{0,2,1:T(8,128)(2,1)} copy(bf16[2048,1,1002]{2,0,1:T(8,128)(2,1)} %convert_bitcast_fusion) | data formatting | bytes 8208384
  541.9 0.0 copy-done.1
  (1 shorter events, 0.0 us)
Async XLA Ops:
  7.2 38.7 %copy-start = (bf16[512,2048]{1,0:T(8,128)(2,1)S(1)}, bf16[512,2048]{1,0:T(8,128)(2,1)}, u32[]{:S(2)}) copy-start(bf16[512,2048]{1,0:T(8,128)(2,1)} %param.3) | copy-start | bytes 6291460
  7.2 30.6 %all-gather.2.cloned.1.call-start = ((), (), s32[]{:S(2)}) async-start(), calls=%async_computation.1 | async-start | bytes 12386304 | tf_op jit(solution)/shard_map/all_gather | solution.py:13
  7.9 143.7 %all-reduce.6.cloned.1.call-start = ((), (), s32[]{:S(2)}) async-start(), calls=%async_computation.2 | async-start | bytes 8224768 | tf_op jit(solution)/shard_map/psum | solution.py:17
  54.7 474.6 %reduce-scatter.2.cloned.1.call-start = ((), (), s32[]{:S(2)}) async-start(), calls=%async_computation.3 | async-start | bytes 25165824 | tf_op jit(solution)/shard_map/reduce_scatter | solution.py:40
  345.3 1.6 copy-start.2
  529.3 12.6 %copy-start.1 = (bf16[512,2048]{1,0:T(8,128)(2,1)S(1)}, bf16[512,2048]{1,0:T(8,128)(2,1)}, u32[]{:S(2)}) copy-start(bf16[512,2048]{1,0:T(8,128)(2,1)} %param.3) | copy-start | bytes 6291460
Sparse Core Ops, SparseCore 0:
  9.8 27.9 all-gather.1
  54.8 96.8 all-reduce.5
  345.5 27.6 reduce-scatter.1
where the time goes:
time: 549 us; the launch traced here: 548 us
  blocking collectives  317 us (58%)
  waiting for transfers between devices  115 us (21%)
  local copies, waits for them, and re-layouts  46 us (8%)
  other arithmetic  28.1 us (5%)
  matrix products  27.7 us (5%)
  between operations  13.8 us (3%)
    psum x2, blocking collectives, body(): lax.psum((jnp.sum(jnp.exp(student - student_peak[:, None]), axis=1), jnp....  242 us
    psum x1, waiting for transfers between devices, body(): student = lax.psum(partial_value, 'width')  84.9 us
    pmax x1, blocking collectives, body(): student_peak, target_peak = lax.pmax((student_peak, target_peak), 'vocab')  75.3 us
    all_gather x1, waiting for transfers between devices, body(): lax.all_gather(head, 'dp', axis=1, tiled=True)  29.8 us
    transpose x1, local copies, waits for them, and re-layouts, body(): jnp.einsum('td,tkv->kdv', hidden, grad_blocks, preferred_element_type=jnp...  17.9 us
  transfers between devices with their start and end apart: 3, of which 2 were waited for; matrix products, arithmetic and copies ran while one was open for 4% of the time, Pallas kernels for 0%

commit v1 on v0

--- a/solution.py
+++ b/solution.py
@@ -14,7 +14,9 @@
         width_cols, halves * local_cols
     )
     partial_value = jnp.dot(hidden, full_head, preferred_element_type=jnp.float32)
-    student = lax.psum(partial_value, "width")
+    student = partial_value
+    for hop in (1, 2):
+        student = student + lax.ppermute(student, "width", [(dev, dev ^ hop) for dev in range(4)])
     target = teacher.reshape(tok_rows, halves * local_cols).astype(jnp.float32)
     student_peak = jnp.max(student, axis=1)
     target_peak = jnp.max(target, axis=1)

time: 549 us -> 640 us (1.17)
  waiting for transfers between devices: 115 us -> 200 us
  other arithmetic: 28.1 us -> 34.7 us
    ppermute x0 -> x2, waiting for transfers between devices: none -> 170 us  [body(): lax.ppermute(student, 'width', [(dev, dev ^ hop) for dev in range(4)])]
    psum x1 -> x0, waiting for transfers between devices: 84.9 us -> none  [body(): student = lax.psum(partial_value, 'width')]
  transfers between devices with their start and end apart: 3 -> 4, of which waited for: 2 -> 3; matrix products, arithmetic and copies ran while one was open for 4% -> 3% of each run, Pallas kernels for 0% -> 0%
where the time goes in v1:
time: 640 us; the launch traced here: 639 us
  blocking collectives  317 us (50%)
  waiting for transfers between devices  200 us (31%)
  local copies, waits for them, and re-layouts  44.5 us (7%)
  other arithmetic  34.7 us (5%)
  matrix products  25.8 us (4%)
  between operations  14.1 us (2%)
    psum x2, blocking collectives, body(): lax.psum((jnp.sum(jnp.exp(student - student_peak[:, None]), axis=1), jnp....  242 us
    ppermute x2, waiting for transfers between devices, body(): lax.ppermute(student, 'width', [(dev, dev ^ hop) for dev in range(4)])  170 us
    pmax x1, blocking collectives, body(): student_peak, target_peak = lax.pmax((student_peak, target_peak), 'vocab')  75.3 us
    all_gather x1, waiting for transfers between devices, body(): lax.all_gather(head, 'dp', axis=1, tiled=True)  29.8 us
    transpose x1, local copies, waits for them, and re-layouts, body(): jnp.einsum('td,tkv->kdv', hidden, grad_blocks, preferred_element_type=jnp...  17.9 us
  transfers between devices with their start and end apart: 4, of which 3 were waited for; matrix products, arithmetic and copies ran while one was open for 3% of the time, Pallas kernels for 0%

profile of v1, /device:TPU:2, one launch (start us, length us, event | category | flops | bytes accessed | tf_op | source)
XLA Modules:
  0.0 639.4 jit_solution(215737727800877284)
XLA Ops:
  7.2 0.0 copy-start
  7.2 0.0 all-gather.2.cloned.1.call-start
  7.2 0.7 all-gather.2.cloned.1.call-update
  7.9 0.0 reduce-scatter.2.cloned.1.call-start
  8.0 29.8 %all-gather.2.cloned.1.call-done = bf16[2048,2,1002]{0,2,1:T(8,128)(2,1)} async-done(((bf16[2048,1,1002]{0,2,1:T(8,128)(2,1)}), bf16[2048,2,1002]{0,2,1:T(8,128)(2,1)}) %all-gather.2.cloned.1.call-update) | async-done | bytes 8208400 | tf_op jit(solution)/shard_map/all_gather | solution.py:13
  37.8 8.1 %reshape.29 = bf16[2048,2004]{0,1:T(8,128)(2,1)} reshape(bf16[2048,2,1002]{0,2,1:T(8,128)(2,1)} %all-gather.2.cloned.1.call-done) | data formatting | bytes 16416768 | tf_op jit(solution)/shard_map/reshape | solution.py:13
  45.9 0.0 copy-done
  45.9 6.9 %fusion.2 = f32[512,2004]{0,1:T(8,128)S(1)} fusion(bf16[512,2048]{1,0:T(8,128)(2,1)S(1)} %copy-done, bf16[2048,2004]{0,1:T(8,128)(2,1)} %reshape.29), kind=kOutput, calls=%fused_computation.11 | convolution fusion | flops 4202692608 | bytes 14409728 | tf_op jit(solution)/shard_map/dot_general | solution.py:16
  52.8 0.0 copy-start.2
  52.8 0.9 collective-permute-start
  53.7 90.2 %collective-permute-done = f32[512,2004]{0,1:T(8,128)S(1)} collective-permute-done((f32[512,2004]{0,1:T(8,128)S(1)}, f32[512,2004]{0,1:T(8,128)S(1)}, u32[]{:S(2)}, u32[]{:S(2)}) %collective-permute-start) | collective-permute-done | bytes 4104224 | tf_op jit(solution)/shard_map/ppermute | solution.py:19
  143.9 2.9 add.25
  146.8 2.1 collective-permute-start.1
  148.9 0.0 copy-done.2
  148.9 2.6 copy.13
  151.5 3.3 reduce_max.23
  154.8 4.5 reshape.33
  159.3 79.4 %collective-permute-done.1 = f32[512,2004]{0,1:T(8,128)} collective-permute-done((f32[512,2004]{0,1:T(8,128)}, f32[512,2004]{0,1:T(8,128)}, u32[]{:S(2)}, u32[]{:S(2)}) %collective-permute-start.1) | collective-permute-done | bytes 4104224 | tf_op jit(solution)/shard_map/ppermute | solution.py:19
  238.8 6.1 fusion.1
  244.9 75.3 %all-reduce.2 = (f32[512]{0:T(512)S(1)}, f32[512]{0:T(512)S(1)}) all-reduce(f32[512]{0:T(512)S(1)} %get-tuple-element.20, bf16[512]{0:T(512)(128)(2,1)S(1)} %reduce_max.23), channel_id=1, replica_groups=mesh['dp'=2,'width'=4,'vocab'=32] {'vocab'}, use_global_device_ids=true, to_apply=%region_7.0 | all-reduce | flops 1024 | bytes 7168 | tf_op jit(solution)/shard_map/pmax | solution.py:23
  320.2 4.9 exponential_reduce_fusion.1
  325.0 4.8 multiply_reduce_fusion
  329.8 69.6 %all-reduce.1 = (f32[512]{0:T(512)S(1)}, f32[512]{0:T(512)S(1)}) all-reduce(f32[512]{0:T(512)S(1)} %get-tuple-element.13, f32[512]{0:T(512)S(1)} %exponential_reduce_fusion.1), channel_id=1, replica_groups=mesh['dp'=2,'width'=4,'vocab'=32] {'vocab'}, use_global_device_ids=true, to_apply=%region_9.0 | all-reduce | flops 1024 | bytes 8192 | tf_op jit(solution)/shard_map/psum | solution.py:25
  399.4 6.0 multiply_convert_fusion
  405.4 3.3 reshape.30
  408.7 9.5 %convolution_bitcast_fusion = f32[2,2048,1002]{1,2,0:T(8,128)} fusion(bf16[512,2,1002]{0,2,1:T(8,128)(2,1)} %reshape.30, bf16[512,2048]{1,0:T(8,128)(2,1)S(1)} %copy-done), kind=kOutput, calls=%fused_computation | convolution fusion | flops 4202692608 | bytes 20566016 | tf_op jit(solution)/shard_map/td,tkv->kdv/dot_general | solution.py:41
  418.2 17.9 %copy.14 = f32[2,2048,1002]{2,1,0:T(8,128)} copy(f32[2,2048,1002]{1,2,0:T(8,128)} %convolution_bitcast_fusion) | data formatting | bytes 32833536 | tf_op jit(solution)/shard_map/td,tkv->kdv/transpose | solution.py:41
  436.1 0.0 copy-start.3
  436.1 0.0 reduce-scatter.2.cloned.1.call-update
  436.1 1.6 copy-done.3
  437.7 9.5 %fusion.3 = f32[512,2048]{1,0:T(8,128)} fusion(bf16[512,2004]{0,1:T(8,128)(2,1)S(1)} %copy-done.3, bf16[2048,2004]{0,1:T(8,128)(2,1)} %reshape.29), kind=kOutput, calls=%fused_computation.12 | convolution fusion | flops 4202692608 | bytes 14454784 | tf_op jit(solution)/shard_map/dot_general | solution.py:46
  447.1 172.2 %all-reduce.4 = (f32[512]{0:T(512)S(1)}, bf16[512,2048]{1,0:T(8,128)(2,1)}) all-reduce(f32[512]{0:T(512)S(1)} %get-tuple-element.12, f32[512,2048]{1,0:T(8,128)} %fusion.3), channel_id=1, replica_groups=mesh['dp'=2,'width'=4,'vocab'=32] {'vocab'}, use_global_device_ids=true, to_apply=%region_3.0 | all-reduce | flops 1049088 | bytes 6295552 | tf_op jit(solution)/shard_map/psum | solution.py:25
  619.4 0.6 subtract_add_fusion
  620.0 0.0 reduce-scatter.2.cloned.1.call-done
  620.0 0.0 copy-start.1
  620.0 6.1 convert_bitcast_fusion
  626.1 6.5 %copy.15 = bf16[2048,1,1002]{0,2,1:T(8,128)(2,1)} copy(bf16[2048,1,1002]{2,0,1:T(8,128)(2,1)} %convert_bitcast_fusion) | data formatting | bytes 8208384
  632.6 0.0 copy-done.1
  (1 shorter events, 0.0 us)
Async XLA Ops:
  7.2 38.7 %copy-start = (bf16[512,2048]{1,0:T(8,128)(2,1)S(1)}, bf16[512,2048]{1,0:T(8,128)(2,1)}, u32[]{:S(2)}) copy-start(bf16[512,2048]{1,0:T(8,128)(2,1)} %param.3) | copy-start | bytes 6291460
  7.2 30.6 %all-gather.2.cloned.1.call-start = ((), (), s32[]{:S(2)}) async-start(), calls=%async_computation.1 | async-start | bytes 12386304 | tf_op jit(solution)/shard_map/all_gather | solution.py:13
  7.9 612.1 %reduce-scatter.2.cloned.1.call-start = ((), (), s32[]{:S(2)}) async-start(), calls=%async_computation.2 | async-start | bytes 25165824 | tf_op jit(solution)/shard_map/reduce_scatter | solution.py:42
  52.8 96.1 %copy-start.2 = (bf16[512,2,1002]{0,1,2:T(2,128)(2,1)S(1)}, bf16[512,2,1002]{0,1,2:T(2,128)(2,1)}, u32[]{:S(2)}) copy-start(bf16[512,2,1002]{0,1,2:T(2,128)(2,1)} %param.5) | copy-start | bytes 6156292
  52.8 91.1 %collective-permute-start = (f32[512,2004]{0,1:T(8,128)S(1)}, f32[512,2004]{0,1:T(8,128)S(1)}, u32[]{:S(2)}, u32[]{:S(2)}) collective-permute-start(f32[512,2004]{0,1:T(8,128)S(1)} %fusion.2), channel_id=1, source_target_pairs={{0,32},{32,0},{64,96},{96,64},{1,33},{33,1},{65,97},{97,65},{2,34}... | collective-permute-start | bytes 12312584 | tf_op jit(solution)/shard_map/ppermute | solution.py:19
  146.8 92.0 %collective-permute-start.1 = (f32[512,2004]{0,1:T(8,128)}, f32[512,2004]{0,1:T(8,128)}, u32[]{:S(2)}, u32[]{:S(2)}) collective-permute-start(f32[512,2004]{0,1:T(8,128)} %add.25), channel_id=1, source_target_pairs={{0,64},{32,96},{64,0},{96,32},{1,65},{33,97},{65,1},{97,33},{2,66}... | collective-permute-start | bytes 12312584 | tf_op jit(solution)/shard_map/ppermute | solution.py:19
  436.1 1.6 copy-start.3
  620.0 12.6 %copy-start.1 = (bf16[512,2048]{1,0:T(8,128)(2,1)S(1)}, bf16[512,2048]{1,0:T(8,128)(2,1)}, u32[]{:S(2)}) copy-start(bf16[512,2048]{1,0:T(8,128)(2,1)} %param.3) | copy-start | bytes 6291460
Sparse Core Ops, SparseCore 0:
  9.8 27.9 all-gather.1
  436.2 27.9 reduce-scatter.1
